TPU v7x, 32 devices: a whole 2x2x4 slice. The times are simulated.
32 devices in a mesh: shard: 2 (over y), ctx: 4 (over z), tp: 4 (over x, core).
Axes of the slice: x: 2, y: 2, z: 4, core: 2. Of those that a mesh axis runs over, the one named last changes fastest.
Arguments:
- inputs: bfloat16 [4, 1024, 768], P('shard', ('ctx', 'tp')), may hold values from -6 to 6
- seg_ids: int32 [4, 1024], P('shard', 'ctx'), may hold values from 0 to 7, never falling along the last dimension, each value on 1 to 512 neighbouring positions
- feature_map: float32 [12, 64, 256], P('tp'), may hold values from -6 to 6
- w_query: bfloat16 [768, 768], P(('shard', 'ctx'), 'tp'), may hold values from -0.21875 to 0.21875
- w_key: bfloat16 [768, 768], P(('shard', 'ctx'), 'tp'), may hold values from -0.21875 to 0.21875
- w_value: bfloat16 [768, 768], P(('shard', 'ctx'), 'tp'), may hold values from -0.21875 to 0.21875
- w_out: bfloat16 [768, 768], P('tp', ('shard', 'ctx')), may hold values from -0.875 to 0.875
- gain_attn: float32 [768], replicated, may hold values from 0.5 to 1.5
- shift_attn: float32 [768], replicated, may hold values from -3 to 3
- w_up: bfloat16 [768, 3072], P(('shard', 'ctx'), 'tp'), may hold values from -0.21875 to 0.21875
- bias_up: float32 [3072], P('tp'), may hold values from -3 to 3
- w_down: bfloat16 [3072, 768], P('tp', ('shard', 'ctx')), may hold values from -0.109375 to 0.109375
- bias_down: float32 [768], replicated, may hold values from -3 to 3
- gain_ffn: float32 [768], replicated, may hold values from 0.5 to 1.5
- shift_ffn: float32 [768], replicated, may hold values from -3 to 3
- cotangent: bfloat16 [4, 1024, 768], P('shard', ('ctx', 'tp')), may hold values from -6 to 6
Outputs:
- outputs: bfloat16 [4, 1024, 768], P('shard', ('ctx', 'tp'))
- grad_inputs: bfloat16 [4, 1024, 768], P('shard', ('ctx', 'tp'))
- grad_query: float32 [768, 768], P(('shard', 'ctx'), 'tp')
- grad_key: float32 [768, 768], P(('shard', 'ctx'), 'tp')
- grad_value: float32 [768, 768], P(('shard', 'ctx'), 'tp')
- grad_out: float32 [768, 768], P('tp', ('shard', 'ctx'))
- grad_gain_attn: float32 [768], replicated
- grad_shift_attn: float32 [768], replicated
- grad_up: float32 [768, 3072], P(('shard', 'ctx'), 'tp')
- grad_bias_up: float32 [3072], P('tp')
- grad_down: float32 [3072, 768], P('tp', ('shard', 'ctx'))
- grad_bias_down: float32 [768], replicated
- grad_gain_ffn: float32 [768], replicated
- grad_shift_ffn: float32 [768], replicated
Inputs may be any that keep to these rules, and one draw needn't show every extreme that they name: `seg_ids`: within each sequence the numbers never fall, every number below 8 occurs, and no document has more than 512 tokens.
All inputs are finite; a program needn't handle non-finite values.
Results may differ from a plain program's by a relative error of at most 0.025.
Values may be sent and summed in bfloat16 or wider, within the bound.
A program may use at most 128 MiB of HBM per device.

v0:
```python
import jax
import jax.numpy as jnp
from jax import lax
from jax.sharding import PartitionSpec as P

HEAD_DIM = 64
FEATS = 256
FF = 3072
SEGS = 8
highest = lax.Precision.HIGHEST
root_half = 0.7071067811865476
inv_root_tau = 0.3989422804014327
norm_eps = 1e-05


def gelu_value(upper):
    return upper * 0.5 * (1.0 + lax.erf(upper * root_half))


def gelu_slope(upper):
    return 0.5 * (1.0 + lax.erf(upper * root_half)) + upper * inv_root_tau * jnp.exp(
        -0.5 * upper * upper
    )


def layer_norm(hidden_in, gain_vec, shift_vec):
    mean_val = jnp.mean(hidden_in, -1, keepdims=True)
    centred = hidden_in - mean_val
    inv_std = lax.rsqrt(jnp.mean(centred * centred, -1, keepdims=True) + norm_eps)
    normed = centred * inv_std
    return (normed * gain_vec + shift_vec, normed, inv_std)


def norm_back(grad_in, normed, inv_std, gain_vec):
    scaled = grad_in * gain_vec
    grad_hidden = inv_std * (
        scaled
        - jnp.mean(scaled, -1, keepdims=True)
        - normed * jnp.mean(scaled * normed, -1, keepdims=True)
    )
    return (grad_hidden, jnp.sum(grad_in * normed, (0, 1)), jnp.sum(grad_in, (0, 1)))


def features(projected, omega_local):
    seq_count, ctx_rows, width = projected.shape
    heads_here = omega_local.shape[0]
    scaled = projected.reshape(seq_count, ctx_rows, heads_here, HEAD_DIM) * HEAD_DIM ** (-0.25)
    angles = jnp.einsum("schd,hdm->schm", scaled, omega_local, precision=highest)
    squares = 0.5 * jnp.sum(scaled * scaled, -1, keepdims=True)
    return (jnp.exp(angles - squares) * FEATS ** (-0.5), scaled)


def feature_back(grad_phi, phi_full, scaled, omega_local):
    grad_angle = grad_phi * phi_full
    grad_scaled = jnp.einsum("schm,hdm->schd", grad_angle, omega_local, precision=highest)
    grad_scaled = grad_scaled - scaled * jnp.sum(grad_angle, -1, keepdims=True)
    seq_count, ctx_rows, heads_here, head_width = scaled.shape
    return (grad_scaled * HEAD_DIM ** (-0.25)).reshape(seq_count, ctx_rows, heads_here * head_width)


def spread_rows(mask_low, left):
    ctx_rows, heads_here, feat_count = left.shape
    wide = mask_low[:, None, :, None] * left[:, :, None, :]
    return wide.reshape(ctx_rows, heads_here, -1)


def segment_outer(operands):
    mask_low, left, right = operands
    return jnp.einsum(
        "chx,che->hxe", spread_rows(mask_low, left), right, preferred_element_type=jnp.float32
    )


def segment_apply(operands):
    mask_low, left, table = operands
    return jnp.einsum(
        "chx,hxe->che", spread_rows(mask_low, left), table, preferred_element_type=jnp.float32
    )


def segment_back(operands):
    mask_full, left, table = operands
    ctx_rows, heads_here, width = left.shape
    seg_count = mask_full.shape[1]
    wide = jnp.einsum("che,hxe->chx", left, table, preferred_element_type=jnp.float32)
    wide = wide.reshape(ctx_rows, heads_here, seg_count, -1)
    return jnp.sum(wide * mask_full[:, None, :, None], 2)


def inner_product(left, right):
    return lax.dot_general(
        left, right, (((0,), (0,)), ((), ())), preferred_element_type=jnp.float32
    )


def right_transposed(left, right):
    return lax.dot_general(
        left, right, (((1,), (1,)), ((), ())), preferred_element_type=jnp.float32
    )


def per_device(
    inputs,
    seg_ids,
    feature_map,
    w_query,
    w_key,
    w_value,
    w_out,
    gain_attn,
    shift_attn,
    w_up,
    bias_up,
    w_down,
    bias_down,
    gain_ffn,
    shift_ffn,
    cotangent,
):
    full_query, full_key, full_value, full_up, full_out, full_down = (
        lax.all_gather(w_query, ("shard", "ctx"), axis=0, tiled=True),
        lax.all_gather(w_key, ("shard", "ctx"), axis=0, tiled=True),
        lax.all_gather(w_value, ("shard", "ctx"), axis=0, tiled=True),
        lax.all_gather(w_up, ("shard", "ctx"), axis=0, tiled=True),
        lax.all_gather(w_out, ("shard", "ctx"), axis=1, tiled=True),
        lax.all_gather(w_down, ("shard", "ctx"), axis=1, tiled=True),
    )
    seq_count, row_share, width = inputs.shape
    rows_all = lax.all_gather(inputs, "tp", axis=1, tiled=True)
    ctx_rows = rows_all.shape[1]
    token_count = seq_count * ctx_rows
    flat = rows_all.reshape(token_count, width)
    heads_here = feature_map.shape[0]
    head_cols = heads_here * HEAD_DIM
    query_proj = jnp.dot(flat, full_query, preferred_element_type=jnp.float32).reshape(
        seq_count, ctx_rows, head_cols
    )
    key_proj = jnp.dot(flat, full_key, preferred_element_type=jnp.float32).reshape(
        seq_count, ctx_rows, head_cols
    )
    value_low = jnp.dot(flat, full_value, preferred_element_type=jnp.float32).astype(jnp.bfloat16)
    value_low = value_low.reshape(seq_count, ctx_rows, head_cols)
    value_four = value_low.reshape(seq_count, ctx_rows, heads_here, HEAD_DIM)
    phi_query, scaled_query = features(query_proj, feature_map)
    phi_key, scaled_key = features(key_proj, feature_map)
    phq_low = phi_query.astype(jnp.bfloat16)
    phk_low = phi_key.astype(jnp.bfloat16)
    matches = seg_ids[:, :, None] == jnp.arange(SEGS, dtype=jnp.int32)[None, None, :]
    mask_low = matches.astype(jnp.bfloat16)
    mask_full = matches.astype(jnp.float32)
    kv_part = lax.map(segment_outer, (mask_low, phk_low, value_four))
    z_part = jnp.einsum("scg,schm->shgm", mask_low, phk_low, preferred_element_type=jnp.float32)
    kv_sum, z_sum = lax.psum((kv_part, z_part), "ctx")
    kv_low = kv_sum.astype(jnp.bfloat16)
    numer = lax.map(segment_apply, (mask_low, phq_low, kv_low))
    phq_wide = phq_low.astype(jnp.float32)
    denom = jnp.sum(
        jnp.einsum("schm,shgm->schg", phq_wide, z_sum, precision=highest)
        * mask_full[:, :, None, :],
        -1,
    )
    mixed = numer / denom[..., None]
    mixed_low = mixed.astype(jnp.bfloat16).reshape(seq_count, ctx_rows, head_cols)
    piece = mixed_low
    attn_sum = jnp.swapaxes(
        lax.psum_scatter(
            jnp.einsum("scf,fd->csd", piece, full_out, preferred_element_type=jnp.float32),
            "tp",
            scatter_dimension=0,
            tiled=True,
        ),
        0,
        1,
    )
    first, normed_one, inv_one = layer_norm(
        inputs.astype(jnp.float32) + attn_sum, gain_attn, shift_attn
    )
    first_low = first.astype(jnp.bfloat16)
    first_rows = lax.all_gather(first_low, "tp", axis=1, tiled=True)
    first_flat = first_rows.reshape(token_count, width)
    upper = jnp.dot(first_flat, full_up, preferred_element_type=jnp.float32) + bias_up
    ffn_here = upper.shape[1]
    hidden_low = gelu_value(upper).astype(jnp.bfloat16)
    hidden_three = hidden_low.reshape(seq_count, ctx_rows, ffn_here)
    piece = hidden_three
    branch = jnp.swapaxes(
        lax.psum_scatter(
            jnp.einsum("scf,fd->csd", piece, full_down, preferred_element_type=jnp.float32),
            "tp",
            scatter_dimension=0,
            tiled=True,
        ),
        0,
        1,
    )
    final, normed_two, inv_two = layer_norm(first + branch + bias_down, gain_ffn, shift_ffn)
    outputs = final.astype(jnp.bfloat16)
    full_query, full_key, full_value, full_up, full_out, full_down = (
        lax.all_gather(w_query, ("shard", "ctx"), axis=0, tiled=True),
        lax.all_gather(w_key, ("shard", "ctx"), axis=0, tiled=True),
        lax.all_gather(w_value, ("shard", "ctx"), axis=0, tiled=True),
        lax.all_gather(w_up, ("shard", "ctx"), axis=0, tiled=True),
        lax.all_gather(w_out, ("shard", "ctx"), axis=1, tiled=True),
        lax.all_gather(w_down, ("shard", "ctx"), axis=1, tiled=True),
    )
    grad_final = cotangent.astype(jnp.float32)
    grad_two, grad_gain_ffn, grad_shift_ffn = norm_back(grad_final, normed_two, inv_two, gain_ffn)
    grad_bias_down = jnp.sum(grad_two, (0, 1))
    grad_two_rows = lax.all_gather(grad_two.astype(jnp.bfloat16), "tp", axis=1, tiled=True)
    grad_two_flat = grad_two_rows.reshape(token_count, width)
    grad_hidden = right_transposed(grad_two_flat, full_down)
    grad_upper = (grad_hidden * gelu_slope(upper)).astype(jnp.bfloat16)
    grad_down = inner_product(hidden_low, grad_two_flat)
    grad_up = inner_product(first_flat, grad_upper)
    grad_bias_local = jnp.sum(grad_upper.astype(jnp.float32), 0)
    grad_upper_three = grad_upper.reshape(seq_count, ctx_rows, ffn_here)
    piece = grad_upper_three
    grad_first = grad_two + jnp.swapaxes(
        lax.psum_scatter(
            jnp.einsum("scf,df->csd", piece, full_up, preferred_element_type=jnp.float32),
            "tp",
            scatter_dimension=0,
            tiled=True,
        ),
        0,
        1,
    )
    grad_one, grad_gain_attn, grad_shift_attn = norm_back(
        grad_first, normed_one, inv_one, gain_attn
    )
    grad_one_rows = lax.all_gather(grad_one.astype(jnp.bfloat16), "tp", axis=1, tiled=True)
    grad_one_flat = grad_one_rows.reshape(token_count, width)
    grad_out = inner_product(mixed_low.reshape(token_count, head_cols), grad_one_flat)
    grad_mixed = right_transposed(grad_one_flat, full_out).reshape(
        seq_count, ctx_rows, heads_here, HEAD_DIM
    )
    grad_numer = (grad_mixed / denom[..., None]).astype(jnp.bfloat16)
    grad_denom = -jnp.sum(grad_mixed * mixed, -1) / denom
    kv_grad_part = lax.map(segment_outer, (mask_low, phq_low, grad_numer))
    z_grad_part = jnp.einsum(
        "scg,schm->shgm", mask_full, phq_wide * grad_denom[..., None], precision=highest
    )
    kv_grad, z_grad = (
        lax.psum(kv_grad_part.astype(jnp.bfloat16), "ctx").astype(jnp.float32),
        lax.psum(z_grad_part.astype(jnp.bfloat16), "ctx").astype(jnp.float32),
    )
    kv_grad_low = kv_grad.astype(jnp.bfloat16)
    grad_phq = lax.map(segment_back, (mask_full, grad_numer, kv_low))
    grad_phq = grad_phq + grad_denom[..., None] * jnp.einsum(
        "scg,shgm->schm", mask_full, z_sum, precision=highest
    )
    grad_phk = lax.map(segment_back, (mask_full, value_four, kv_grad_low))
    grad_phk = grad_phk + jnp.einsum("scg,shgm->schm", mask_full, z_grad, precision=highest)
    grad_value_rows = lax.map(segment_apply, (mask_low, phk_low, kv_grad_low)).astype(jnp.bfloat16)
    grad_value_rows = grad_value_rows.reshape(seq_count, ctx_rows, head_cols)
    grad_query_rows = feature_back(grad_phq, phi_query, scaled_query, feature_map).astype(
        jnp.bfloat16
    )
    grad_key_rows = feature_back(grad_phk, phi_key, scaled_key, feature_map).astype(jnp.bfloat16)
    grad_query = inner_product(flat, grad_query_rows.reshape(token_count, head_cols))
    grad_key = inner_product(flat, grad_key_rows.reshape(token_count, head_cols))
    grad_value = inner_product(flat, grad_value_rows.reshape(token_count, head_cols))
    total = jnp.einsum(
        "scf,df->csd", grad_query_rows, full_query, preferred_element_type=jnp.float32
    )
    total = total + jnp.einsum(
        "scf,df->csd", grad_key_rows, full_key, preferred_element_type=jnp.float32
    )
    grad_rows = jnp.swapaxes(
        lax.psum_scatter(
            (
                total
                + jnp.einsum(
                    "scf,df->csd", grad_value_rows, full_value, preferred_element_type=jnp.float32
                )
            ).astype(jnp.bfloat16),
            "tp",
            scatter_dimension=0,
            tiled=True,
        ).astype(jnp.float32),
        0,
        1,
    )
    grad_inputs = (grad_one + grad_rows).astype(jnp.bfloat16)
    grad_query, grad_key, grad_value, grad_up, grad_out, grad_down = (
        lax.psum_scatter(grad_query, ("shard", "ctx"), scatter_dimension=0, tiled=True),
        lax.psum_scatter(grad_key, ("shard", "ctx"), scatter_dimension=0, tiled=True),
        lax.psum_scatter(grad_value, ("shard", "ctx"), scatter_dimension=0, tiled=True),
        lax.psum_scatter(grad_up, ("shard", "ctx"), scatter_dimension=0, tiled=True),
        lax.psum_scatter(grad_out, ("shard", "ctx"), scatter_dimension=1, tiled=True),
        lax.psum_scatter(grad_down, ("shard", "ctx"), scatter_dimension=1, tiled=True),
    )
    tp_index = lax.axis_index("tp")
    padded_bias = lax.dynamic_update_slice(
        jnp.zeros((FF,), jnp.float32), grad_bias_local, (tp_index * ffn_here,)
    )
    grad_gain_attn, grad_shift_attn, grad_gain_ffn, grad_shift_ffn, grad_bias_down, padded_bias = (
        lax.psum(
            (
                grad_gain_attn,
                grad_shift_attn,
                grad_gain_ffn,
                grad_shift_ffn,
                grad_bias_down,
                padded_bias,
            ),
            ("shard", "ctx", "tp"),
        )
    )
    grad_bias_up = lax.dynamic_slice(padded_bias, (tp_index * ffn_here,), (ffn_here,))
    return (
        outputs,
        grad_inputs,
        grad_query,
        grad_key,
        grad_value,
        grad_out,
        grad_gain_attn,
        grad_shift_attn,
        grad_up,
        grad_bias_up,
        grad_down,
        grad_bias_down,
        grad_gain_ffn,
        grad_shift_ffn,
    )


def solution(mesh):
    placed = (
        P("shard", ("ctx", "tp"), None),
        P("shard", "ctx"),
        P("tp", None, None),
        P(("shard", "ctx"), "tp"),
        P(("shard", "ctx"), "tp"),
        P(("shard", "ctx"), "tp"),
        P("tp", ("shard", "ctx")),
        P(),
        P(),
        P(("shard", "ctx"), "tp"),
        P("tp"),
        P("tp", ("shard", "ctx")),
        P(),
        P(),
        P(),
        P("shard", ("ctx", "tp"), None),
    )
    return jax.shard_map(
        per_device,
        mesh=mesh,
        in_specs=placed,
        out_specs=(
            P("shard", ("ctx", "tp"), None),
            P("shard", ("ctx", "tp"), None),
            P(("shard", "ctx"), "tp"),
            P(("shard", "ctx"), "tp"),
            P(("shard", "ctx"), "tp"),
            P("tp", ("shard", "ctx")),
            P(),
            P(),
            P(("shard", "ctx"), "tp"),
            P("tp"),
            P("tp", ("shard", "ctx")),
            P(),
            P(),
            P(),
        ),
        check_vma=False,
    )
```

profile of v0, /device:TPU:0, one launch (start us, length us, event | category | flops | bytes accessed | tf_op | source)
XLA Modules:
  0.0 1010.8 jit_solution(17872332154931087539)
XLA Ops:
  8.1 10.4 %all_gather.36 = bf16[2,256,768]{2,1,0:T(8,128)(2,1)S(1)} all-gather(bf16[2,64,768]{2,1,0:T(8,128)(2,1)} %param.28), channel_id=1, replica_groups=mesh['shard'=2,'ctx'=4,'tp'=4] {'tp'}, dimensions={1}, use_global_device_ids=true | all-gather | bytes 983040 | tf_op jit(solution)/shard_map/all_gather | solution.py:129
  18.5 32.5 %all_gather.37 = bf16[768,192]{1,0:T(8,128)(2,1)S(1)} all-gather(bf16[96,192]{1,0:T(8,128)(2,1)} %param.32), channel_id=1, replica_groups=mesh['shard'=2,'ctx'=4,'tp'=4] {'shard','ctx'}, dimensions={0}, use_global_device_ids=true | all-gather | bytes 331776 | tf_op jit(solution)/shard_map/all_gather | solution.py:122
  56.2 31.6 %all_gather.38 = bf16[768,192]{1,0:T(8,128)(2,1)S(1)} all-gather(bf16[96,192]{1,0:T(8,128)(2,1)S(1)} %copy-done.48), channel_id=1, replica_groups=mesh['shard'=2,'ctx'=4,'tp'=4] {'shard','ctx'}, dimensions={0}, use_global_device_ids=true | all-gather | bytes 331776 | tf_op jit(solution)/shard_map/all_gather | solution.py:123
  92.7 20.8 %while.66 = (s32[]{:T(128)}, f32[2,3,2048,64]{2,3,1,0:T(8,128)}, bf16[2,256,8]{2,1,0:T(8,128)(2,1)S(1)}, bf16[2,256,3,256]{3,1,2,0:T(8,128)(2,1)}, bf16[2,256,3,64]{1,3,2,0:T(8,128)(2,1)}) while((s32[]{:T(128)}, f32[2,3,2048,64]{2,3,1,0:T(8,128)}, bf16[2,256,8]{2,1,0:T(8,128)(2,1)S(1)}, bf16[2,256,3,256]{3,1,2,0:T(8,128)(2,1)}, ...), condition=%wide.region_3.4_spmd.clone, body=%wide.region_2.3_spmd.sunk.clone | while | flops 207618048 | bytes 20427872 | solution.py:151
  113.6 32.0 %all_gather.39 = bf16[768,192]{1,0:T(8,128)(2,1)S(1)} all-gather(bf16[96,192]{1,0:T(8,128)(2,1)S(1)} %copy-done.49), channel_id=1, replica_groups=mesh['shard'=2,'ctx'=4,'tp'=4] {'shard','ctx'}, dimensions={0}, use_global_device_ids=true | all-gather | bytes 331776 | tf_op jit(solution)/shard_map/all_gather | solution.py:121
  152.0 96.4 %all-reduce.6 = (bf16[2,3,2048,64]{2,3,1,0:T(8,128)(2,1)}, f32[2,3,8,256]{3,2,1,0:T(8,128)S(1)}) all-reduce(f32[2,3,2048,64]{2,3,1,0:T(8,128)} %get-tuple-element.176, f32[2,3,8,256]{3,2,1,0:T(8,128)S(1)} %copy-done.46), channel_id=1, replica_groups=mesh['shard'=2,'ctx'=4,'tp'=4] {'ctx'}, use_global_device_ids=true, to_apply=%region_4.5 | all-reduce | flops 798720 | bytes 4816896 | tf_op jit(solution)/shard_map/psum | solution.py:153
  248.4 19.4 %while.67 = (s32[]{:T(128)}, f32[2,256,3,64]{1,3,2,0:T(8,128)}, bf16[2,3,2048,64]{2,3,1,0:T(8,128)(2,1)}, bf16[2,256,8]{2,1,0:T(8,128)(2,1)S(1)}, bf16[2,256,3,256]{3,1,2,0:T(8,128)(2,1)}) while((s32[]{:T(128)}, f32[2,256,3,64]{1,3,2,0:T(8,128)}, bf16[2,3,2048,64]{2,3,1,0:T(8,128)(2,1)}, bf16[2,256,8]{2,1,0:T(8,128)(2,1)S(1)}, ...), condition=%wide.region_6.7_spmd.clone, body=%wide.region_5.6_spmd.sunk.clone | while | flops 202899456 | bytes 31536224 | solution.py:155
  268.7 31.8 %all_gather.40 = bf16[192,768]{0,1:T(8,128)(2,1)S(1)} all-gather(bf16[192,96]{0,1:T(8,128)(2,1)S(1)} %copy.105), channel_id=1, replica_groups=mesh['shard'=2,'ctx'=4,'tp'=4] {'shard','ctx'}, dimensions={1}, use_global_device_ids=true | all-gather | bytes 331776 | tf_op jit(solution)/shard_map/all_gather | solution.py:125
  305.4 27.2 %reduce-scatter.19.cloned.1.call-done = f32[64,2,768]{2,0,1:T(8,128)} async-done(((f32[256,2,768]{2,0,1:T(8,128)}), f32[64,2,768]{2,0,1:T(8,128)}) %reduce-scatter.19.cloned.1.call-update) | async-done | bytes 393232 | tf_op jit(solution)/shard_map/reduce_scatter | solution.py:166
  334.7 8.0 all_gather.41
  351.7 38.5 %all-gather.5.cloned.1.call-done = bf16[768,768]{0,1:T(8,128)(2,1)} async-done(((bf16[768,96]{0,1:T(8,128)(2,1)}), bf16[768,768]{0,1:T(8,128)(2,1)}) %all-gather.5.cloned.1.call-update) | async-done | bytes 1179664 | tf_op jit(solution)/shard_map/all_gather | solution.py:126
  393.6 26.5 %reduce-scatter.21.cloned.1.call-done = f32[64,2,768]{2,0,1:T(8,128)} async-done(((f32[256,2,768]{2,0,1:T(8,128)}), f32[64,2,768]{2,0,1:T(8,128)}) %reduce-scatter.21.cloned.1.call-update) | async-done | bytes 393232 | tf_op jit(solution)/shard_map/reduce_scatter | solution.py:187
  422.0 8.1 all_gather.44
  438.0 25.5 %reduce-scatter.23.cloned.1.call-done = f32[64,2,768]{2,0,1:T(8,128)} async-done(((f32[256,2,768]{2,0,1:T(8,128)}), f32[64,2,768]{2,0,1:T(8,128)}) %reduce-scatter.23.cloned.1.call-update) | async-done | bytes 393232 | tf_op jit(solution)/shard_map/reduce_scatter | solution.py:219
  476.2 20.0 %while.69 = (s32[]{:T(128)}, bf16[2,3,2048,64]{2,3,1,0:T(8,128)(2,1)}, bf16[2,256,8]{2,1,0:T(8,128)(2,1)S(1)}, bf16[2,256,3,256]{3,1,2,0:T(8,128)(2,1)}, bf16[2,256,3,64]{1,3,2,0:T(8,128)(2,1)}) while((s32[]{:T(128)}, bf16[2,3,2048,64]{2,3,1,0:T(8,128)(2,1)}, bf16[2,256,8]{2,1,0:T(8,128)(2,1)S(1)}, ...), condition=%wide.region_26.27_spmd.clone, body=%wide.region_25.26_spmd.sunk.clone | while | flops 207618048 | bytes 20427872 | solution.py:239
  508.3 20.2 %psum.73 = bf16[2,3,8,256]{3,2,1,0:T(8,128)(2,1)S(1)} all-reduce(bf16[2,3,8,256]{3,2,1,0:T(8,128)(2,1)S(1)} %fusion.107), channel_id=1, replica_groups=mesh['shard'=2,'ctx'=4,'tp'=4] {'ctx'}, use_global_device_ids=true, to_apply=%region_31.32 | all-reduce | flops 12288 | bytes 49152 | tf_op jit(solution)/shard_map/psum | solution.py:245
  532.7 33.9 %all-reduce.5.cloned.1.call-done = bf16[2,3,2048,64]{2,3,1,0:T(8,128)(2,1)} async-done(((bf16[2,3,2048,64]{2,3,1,0:T(8,128)(2,1)}), bf16[2,3,2048,64]{2,3,1,0:T(8,128)(2,1)}) %all-reduce.5.cloned.1.call-update) | async-done | bytes 1572880 | tf_op jit(solution)/shard_map/psum | solution.py:244
  580.4 19.7 %while.71 = (s32[]{:T(128)}, bf16[2,256,3,64]{1,3,2,0:T(8,128)(2,1)}, bf16[2,3,2048,64]{2,3,1,0:T(8,128)(2,1)}, bf16[2,256,8]{2,1,0:T(8,128)(2,1)S(1)}, bf16[2,256,3,256]{3,1,2,0:T(8,128)(2,1)}) while((s32[]{:T(128)}, bf16[2,256,3,64]{1,3,2,0:T(8,128)(2,1)}, bf16[2,3,2048,64]{2,3,1,0:T(8,128)(2,1)}, ...), condition=%wide.region_34.35_spmd.clone, body=%wide.region_33.34_spmd.sunk.clone | while | flops 202899456 | bytes 33109144 | solution.py:254
  616.1 40.8 %all-reduce = (f32[768]{0:T(1024)}, f32[768]{0:T(1024)}, f32[3072]{0:T(1024)S(1)}, f32[768]{0:T(1024)}, f32[768]{0:T(1024)}, /*index=5*/f32[768]{0:T(1024)}) all-reduce(f32[768]{0:T(1024)S(1)} %copy-done.69, f32[768]{0:T(1024)S(1)} %copy-done.68, ...), channel_id=1, replica_groups=mesh['shard'=2,'ctx'=4,'tp'=4] {'shard','ctx','tp'}, use_global_device_ids=true, to_apply=%region_41.42 | all-reduce | flops 6912 | bytes 55296 | tf_op jit(solution)/shard_map/psum | solution.py:298
  661.1 63.8 %reduce-scatter.31.cloned.1.call-done = f32[96,192]{1,0:T(8,128)} async-done(((f32[768,192]{1,0:T(8,128)}), f32[96,192]{1,0:T(8,128)}) %reduce-scatter.31.cloned.1.call-update) | async-done | bytes 73744
  724.9 73.0 %reduce-scatter.29.cloned.1.call-done = f32[768,96]{0,1:T(8,128)} async-done(((f32[768,768]{0,1:T(8,128)}), f32[768,96]{0,1:T(8,128)}) %reduce-scatter.29.cloned.1.call-update) | async-done | bytes 294928 | tf_op jit(solution)/shard_map/reduce_scatter | solution.py:291
  797.9 73.1 %reduce-scatter.27.cloned.1.call-done = f32[96,768]{1,0:T(8,128)} async-done(((f32[768,768]{1,0:T(8,128)}), f32[96,768]{1,0:T(8,128)}) %reduce-scatter.27.cloned.1.call-update) | async-done | bytes 294928 | tf_op jit(solution)/shard_map/reduce_scatter | solution.py:289
  871.0 66.2 %reduce-scatter.33.cloned.1.call-done = f32[96,192]{1,0:T(8,128)} async-done(((f32[768,192]{1,0:T(8,128)}), f32[96,192]{1,0:T(8,128)}) %reduce-scatter.33.cloned.1.call-update) | async-done | bytes 73744
  937.2 66.2 %reduce-scatter.35.cloned.1.call-done = f32[96,192]{1,0:T(8,128)} async-done(((f32[768,192]{1,0:T(8,128)}), f32[96,192]{1,0:T(8,128)}) %reduce-scatter.35.cloned.1.call-update) | async-done | bytes 73744
  (366 shorter events, 202.7 us)
Async XLA Ops:
  8.0 44.3 %copy-start = (f32[3,64,256]{2,1,0:T(8,128)S(1)}, f32[3,64,256]{2,1,0:T(8,128)}, u32[]{:S(2)}) copy-start(f32[3,64,256]{2,1,0:T(8,128)} %param.30) | copy-start | bytes 589828
  8.0 324.6 %reduce-scatter.19.cloned.1.call-start = ((), (), s32[]{:S(2)}) async-start(), calls=%async_computation.10 | async-start | bytes 1966080 | tf_op jit(solution)/shard_map/reduce_scatter | solution.py:166
  18.5 69.3 %copy-start.4 = (bf16[2,256,768]{2,1,0:T(8,128)(2,1)}, bf16[2,256,768]{2,1,0:T(8,128)(2,1)S(1)}, u32[]{:S(2)}) copy-start(bf16[2,256,768]{2,1,0:T(8,128)(2,1)S(1)} %all_gather.36) | copy-start | bytes 2359300
  150.7 97.6 %copy-start.24 = (bf16[2,256,3,256]{1,3,0,2:T(8,128)(2,1)}, bf16[2,256,3,256]{1,3,0,2:T(8,128)(2,1)S(1)}, u32[]{:S(2)}) copy-start(bf16[2,256,3,256]{1,3,0,2:T(8,128)(2,1)S(1)} %get-tuple-element.414) | copy-start | bytes 2359300
  304.1 44.3 %all-gather.3.cloned.1.call-start = ((), (), s32[]{:S(2)}) async-start(), calls=%async_computation.11 | async-start | bytes 1327104 | tf_op jit(solution)/shard_map/all_gather | solution.py:124
  304.7 85.5 %all-gather.5.cloned.1.call-start = ((), (), s32[]{:S(2)}) async-start(), calls=%async_computation.12 | async-start | bytes 1327104 | tf_op jit(solution)/shard_map/all_gather | solution.py:126
  305.3 114.8 %reduce-scatter.21.cloned.1.call-start = ((), (), s32[]{:S(2)}) async-start(), calls=%async_computation.13 | async-start | bytes 1966080 | tf_op jit(solution)/shard_map/reduce_scatter | solution.py:187
  333.7 132.5 %copy-start.6 = (f32[2,64,768]{2,1,0:T(8,128)}, f32[2,64,768]{2,1,0:T(8,128)S(1)}, u32[]{:S(2)}) copy-start(f32[2,64,768]{2,1,0:T(8,128)S(1)} %get-tuple-element.395) | copy-start | bytes 1179652
  351.7 41.8 %copy-start.28 = (bf16[512,768]{1,0:T(8,128)(2,1)}, bf16[512,768]{1,0:T(8,128)(2,1)S(1)}, u32[]{:S(2)}) copy-start(bf16[512,768]{1,0:T(8,128)(2,1)S(1)} %get-tuple-element.416) | copy-start | bytes 2359300
  393.5 69.9 %reduce-scatter.23.cloned.1.call-start = ((), (), s32[]{:S(2)}) async-start(), calls=%async_computation.14 | async-start | bytes 1966080 | tf_op jit(solution)/shard_map/reduce_scatter | solution.py:219
  434.8 131.8 %all-reduce.5.cloned.1.call-start = ((), (), s32[]{:S(2)}) async-start(), calls=%async_computation.15 | async-start | bytes 3145728 | tf_op jit(solution)/shard_map/psum | solution.py:244
  496.2 161.4 %reduce-scatter.37.cloned.1.call-start = ((), (), s32[]{:S(2)}) async-start(), calls=%async_computation.22 | async-start | bytes 884736
  531.0 37.0 %copy-start.33 = (bf16[2,256,3,64]{1,3,2,0:T(8,128)(2,1)}, bf16[2,256,3,64]{1,3,2,0:T(8,128)(2,1)S(1)}, u32[]{:S(2)}) copy-start(bf16[2,256,3,64]{1,3,2,0:T(8,128)(2,1)S(1)} %fusion.96) | copy-start | bytes 589828
  532.7 126.6 %reduce-scatter.25.cloned.1.call-start = ((), (), s32[]{:S(2)}) async-start(), calls=%async_computation.16 | async-start | bytes 983040 | tf_op jit(solution)/shard_map/reduce_scatter | solution.py:270
  603.6 121.3 %reduce-scatter.31.cloned.1.call-start = ((), (), s32[]{:S(2)}) async-start(), calls=%async_computation.19 | async-start | bytes 884736
  605.4 192.4 %reduce-scatter.29.cloned.1.call-start = ((), (), s32[]{:S(2)}) async-start(), calls=%async_computation.18 | async-start | bytes 2654208 | tf_op jit(solution)/shard_map/reduce_scatter | solution.py:291
  607.8 263.2 %reduce-scatter.27.cloned.1.call-start = ((), (), s32[]{:S(2)}) async-start(), calls=%async_computation.17 | async-start | bytes 2654208 | tf_op jit(solution)/shard_map/reduce_scatter | solution.py:289
  611.4 325.8 %reduce-scatter.33.cloned.1.call-start = ((), (), s32[]{:S(2)}) async-start(), calls=%async_computation.20 | async-start | bytes 884736
  613.8 389.6 %reduce-scatter.35.cloned.1.call-start = ((), (), s32[]{:S(2)}) async-start(), calls=%async_computation.21 | async-start | bytes 884736
  614.5 44.8 %copy-start.7 = (f32[2,64,768]{2,1,0:T(8,128)S(1)}, f32[2,64,768]{2,1,0:T(8,128)}, u32[]{:S(2)}) copy-start(f32[2,64,768]{2,1,0:T(8,128)} %copy-done.6) | copy-start | bytes 1179652
  614.5 44.8 %copy-start.21 = (f32[2,64,768]{2,1,0:T(8,128)S(1)}, f32[2,64,768]{2,1,0:T(8,128)}, u32[]{:S(2)}) copy-start(f32[2,64,768]{2,1,0:T(8,128)} %copy-done.20) | copy-start | bytes 1179652
  614.5 44.8 %copy-start.55 = (f32[2,64]{1,0:T(2,128)S(1)}, f32[2,64]{1,0:T(2,128)}, u32[]{:S(2)}) copy-start(f32[2,64]{1,0:T(2,128)} %copy-done.52) | copy-start | bytes 1540
  614.5 44.8 %copy-start.75 = (f32[2,64]{1,0:T(2,128)S(1)}, f32[2,64]{1,0:T(2,128)}, u32[]{:S(2)}) copy-start(f32[2,64]{1,0:T(2,128)} %copy-done.74) | copy-start | bytes 1540
  614.5 44.8 %copy-start.77 = (f32[2,64]{1,0:T(2,128)S(1)}, f32[2,64]{1,0:T(2,128)}, u32[]{:S(2)}) copy-start(f32[2,64]{1,0:T(2,128)} %copy-done.76) | copy-start | bytes 1540
  (79 other events, 816.8 us)
Sparse Core Ops, SparseCore 0:
  304.3 28.2 reduce-scatter.18
  393.7 26.3 reduce-scatter.20
  434.9 28.5 reduce-scatter.22
Sparse Core Ops, SparseCore 1:
  306.7 41.7 all-gather.2
  350.4 39.7 all-gather.4
  496.3 70.3 all-reduce.4
  570.0 62.5 reduce-scatter.36
  635.1 22.6 reduce-scatter.24
  661.7 63.1 reduce-scatter.30
  728.8 69.0 reduce-scatter.28
  801.8 69.1 reduce-scatter.26
  874.7 62.4 reduce-scatter.32
  941.1 62.3 reduce-scatter.34
where the time goes:
time: 1020 us; the launch traced here: 1010 us
  waiting for transfers between devices  501 us (49%)
  blocking collectives  320 us (31%)
  local copies, waits for them, and re-layouts  85.6 us (8%)
  matrix products  73.7 us (7%)
  between operations  16.4 us (2%)
  other arithmetic  13 us (1%)
    unnamed x17, waiting for transfers between devices  197 us
    psum x1, blocking collectives, per_device(): kv_sum, z_sum = lax.psum((kv_part, z_part), 'ctx')  96.4 us
    reduce_scatter x1, waiting for transfers between devices, per_device(): lax.psum_scatter(grad_up, ('shard', 'ctx'), scatter_dimension=0, tiled=True)  73.1 us
    reduce_scatter x1, waiting for transfers between devices, per_device(): lax.psum_scatter(grad_down, ('shard', 'ctx'), scatter_dimension=1, tiled=...  73 us
    mul x40, local copies, waits for them, and re-layouts, spread_rows(): wide = mask_low[:, None, :, None] * left[:, :, None, :]  51.8 us
    psum x1, blocking collectives, per_device(): lax.psum((grad_gain_attn, grad_shift_attn, grad_gain_ffn, grad_shift_ffn,...  40.8 us
    all_gather x1, waiting for transfers between devices, per_device(): lax.all_gather(w_down, ('shard', 'ctx'), axis=1, tiled=True)  38.5 us
    psum x1, waiting for transfers between devices, per_device(): lax.psum(kv_grad_part.astype(jnp.bfloat16), 'ctx').astype(jnp.float32)  33.9 us
  transfers between devices with their start and end apart: 13, of which 11 were waited for; matrix products, arithmetic and copies ran while one was open for 7% of the time, Pallas kernels for 0%

commit v1 on v0

--- a/solution.py
+++ b/solution.py
@@ -240,8 +240,12 @@
     z_grad_part = jnp.einsum(
         "scg,schm->shgm", mask_full, phq_wide * grad_denom[..., None], precision=highest
     )
+
+    def load_strips_all_here(a0, bus_axis):
+        return jnp.sum(lax.all_gather(a0, axis_name=bus_axis), axis=0)
+
     kv_grad, z_grad = (
-        lax.psum(kv_grad_part.astype(jnp.bfloat16), "ctx").astype(jnp.float32),
+        load_strips_all_here(kv_grad_part.astype(jnp.bfloat16), "ctx").astype(jnp.float32),
         lax.psum(z_grad_part.astype(jnp.bfloat16), "ctx").astype(jnp.float32),
     )
     kv_grad_low = kv_grad.astype(jnp.bfloat16)

time: 1020 us -> 1080 us (1.059)
  waiting for transfers between devices: 501 us -> 542 us
    all_gather x0 -> x1, waiting for transfers between devices: none -> 76.6 us  [load_strips_all_here(): return jnp.sum(lax.all_gather(a0, axis_name=bus_axis), axis=0)]
    psum x1 -> x0, waiting for transfers between devices: 33.9 us -> none  [per_device(): lax.psum(kv_grad_part.astype(jnp.bfloat16), 'ctx').astype(jnp.float32)]
where the time goes in v1:
time: 1080 us; the launch traced here: 1070 us
  waiting for transfers between devices  542 us (50%)
  blocking collectives  330 us (31%)
  local copies, waits for them, and re-layouts  87.8 us (8%)
  matrix products  72.9 us (7%)
  other arithmetic  17.2 us (2%)
  between operations  16.5 us (2%)
    unnamed x17, waiting for transfers between devices  193 us
    psum x1, blocking collectives, per_device(): kv_sum, z_sum = lax.psum((kv_part, z_part), 'ctx')  96.3 us
    all_gather x1, waiting for transfers between devices, load_strips_all_here(): return jnp.sum(lax.all_gather(a0, axis_name=bus_axis), axis=0)  76.6 us
    reduce_scatter x1, waiting for transfers between devices, per_device(): lax.psum_scatter(grad_up, ('shard', 'ctx'), scatter_dimension=0, tiled=True)  73.1 us
    reduce_scatter x1, waiting for transfers between devices, per_device(): lax.psum_scatter(grad_down, ('shard', 'ctx'), scatter_dimension=1, tiled=...  73 us
    mul x40, local copies, waits for them, and re-layouts, spread_rows(): wide = mask_low[:, None, :, None] * left[:, :, None, :]  51.5 us
    all_gather x1, blocking collectives, per_device(): lax.all_gather(w_out, ('shard', 'ctx'), axis=1, tiled=True)  42.5 us
    psum x1, blocking collectives, per_device(): lax.psum((grad_gain_attn, grad_shift_attn, grad_gain_ffn, grad_shift_ffn,...  39.9 us
  transfers between devices with their start and end apart: 13, of which 11 were waited for; matrix products, arithmetic and copies ran while one was open for 7% of the time, Pallas kernels for 0%

profile of v1, /device:TPU:0, one launch (start us, length us, event | category | flops | bytes accessed | tf_op | source)
XLA Modules:
  0.0 1067.1 jit_solution(2830118090305462046)
XLA Ops:
  8.1 10.4 all_gather.42
  18.5 32.5 %all_gather.43 = bf16[768,192]{1,0:T(8,128)(2,1)S(1)} all-gather(bf16[96,192]{1,0:T(8,128)(2,1)} %param.32), channel_id=1, replica_groups=mesh['shard'=2,'ctx'=4,'tp'=4] {'shard','ctx'}, dimensions={0}, use_global_device_ids=true | all-gather | bytes 331776 | tf_op jit(solution)/shard_map/all_gather | solution.py:122
  56.2 31.6 %all_gather.44 = bf16[768,192]{1,0:T(8,128)(2,1)S(1)} all-gather(bf16[96,192]{1,0:T(8,128)(2,1)S(1)} %copy-done.51), channel_id=1, replica_groups=mesh['shard'=2,'ctx'=4,'tp'=4] {'shard','ctx'}, dimensions={0}, use_global_device_ids=true | all-gather | bytes 331776 | tf_op jit(solution)/shard_map/all_gather | solution.py:123
  92.7 20.7 %while.66 = (s32[]{:T(128)}, f32[2,3,2048,64]{2,3,1,0:T(8,128)}, bf16[2,256,8]{2,1,0:T(8,128)(2,1)S(1)}, bf16[2,256,3,256]{3,1,2,0:T(8,128)(2,1)}, bf16[2,256,3,64]{1,3,2,0:T(8,128)(2,1)}) while((s32[]{:T(128)}, f32[2,3,2048,64]{2,3,1,0:T(8,128)}, bf16[2,256,8]{2,1,0:T(8,128)(2,1)S(1)}, bf16[2,256,3,256]{3,1,2,0:T(8,128)(2,1)}, ...), condition=%wide.region_3.4_spmd.clone, body=%wide.region_2.3_spmd.sunk.clone | while | flops 207618048 | bytes 20427872 | solution.py:151
  113.4 31.9 %all_gather.45 = bf16[768,192]{1,0:T(8,128)(2,1)S(1)} all-gather(bf16[96,192]{1,0:T(8,128)(2,1)S(1)} %copy-done.52), channel_id=1, replica_groups=mesh['shard'=2,'ctx'=4,'tp'=4] {'shard','ctx'}, dimensions={0}, use_global_device_ids=true | all-gather | bytes 331776 | tf_op jit(solution)/shard_map/all_gather | solution.py:121
  151.9 96.3 %all-reduce.3 = (bf16[2,3,2048,64]{2,3,1,0:T(8,128)(2,1)}, f32[2,3,8,256]{3,2,1,0:T(8,128)S(1)}) all-reduce(f32[2,3,2048,64]{2,3,1,0:T(8,128)} %get-tuple-element.176, f32[2,3,8,256]{3,2,1,0:T(8,128)S(1)} %copy-done.49), channel_id=1, replica_groups=mesh['shard'=2,'ctx'=4,'tp'=4] {'ctx'}, use_global_device_ids=true, to_apply=%region_4.5 | all-reduce | flops 798720 | bytes 4816896 | tf_op jit(solution)/shard_map/psum | solution.py:153
  248.3 19.3 %while.67 = (s32[]{:T(128)}, f32[2,256,3,64]{1,3,2,0:T(8,128)}, bf16[2,3,2048,64]{2,3,1,0:T(8,128)(2,1)}, bf16[2,256,8]{2,1,0:T(8,128)(2,1)S(1)}, bf16[2,256,3,256]{3,1,2,0:T(8,128)(2,1)}) while((s32[]{:T(128)}, f32[2,256,3,64]{1,3,2,0:T(8,128)}, bf16[2,3,2048,64]{2,3,1,0:T(8,128)(2,1)}, bf16[2,256,8]{2,1,0:T(8,128)(2,1)S(1)}, ...), condition=%wide.region_6.7_spmd.clone, body=%wide.region_5.6_spmd.sunk.clone | while | flops 202899456 | bytes 31536224 | solution.py:155
  268.5 42.5 %all_gather.46 = bf16[192,768]{0,1:T(8,128)(2,1)S(1)} all-gather(bf16[192,96]{0,1:T(8,128)(2,1)S(1)} %copy.105), channel_id=1, replica_groups=mesh['shard'=2,'ctx'=4,'tp'=4] {'shard','ctx'}, dimensions={1}, use_global_device_ids=true | all-gather | bytes 331776 | tf_op jit(solution)/shard_map/all_gather | solution.py:125
  315.8 27.3 %reduce-scatter.19.cloned.1.call-done = f32[64,2,768]{2,0,1:T(8,128)} async-done(((f32[256,2,768]{2,0,1:T(8,128)}), f32[64,2,768]{2,0,1:T(8,128)}) %reduce-scatter.19.cloned.1.call-update) | async-done | bytes 393232 | tf_op jit(solution)/shard_map/reduce_scatter | solution.py:166
  362.4 38.4 %all-gather.7.cloned.1.call-done = bf16[768,768]{0,1:T(8,128)(2,1)} async-done(((bf16[768,96]{0,1:T(8,128)(2,1)}), bf16[768,768]{0,1:T(8,128)(2,1)}) %all-gather.7.cloned.1.call-update) | async-done | bytes 1179664 | tf_op jit(solution)/shard_map/all_gather | solution.py:126
  404.1 26.5 %reduce-scatter.21.cloned.1.call-done = f32[64,2,768]{2,0,1:T(8,128)} async-done(((f32[256,2,768]{2,0,1:T(8,128)}), f32[64,2,768]{2,0,1:T(8,128)}) %reduce-scatter.21.cloned.1.call-update) | async-done | bytes 393232 | tf_op jit(solution)/shard_map/reduce_scatter | solution.py:187
  432.5 8.1 all_gather.50
  446.9 27.1 %reduce-scatter.23.cloned.1.call-done = f32[64,2,768]{2,0,1:T(8,128)} async-done(((f32[256,2,768]{2,0,1:T(8,128)}), f32[64,2,768]{2,0,1:T(8,128)}) %reduce-scatter.23.cloned.1.call-update) | async-done | bytes 393232 | tf_op jit(solution)/shard_map/reduce_scatter | solution.py:219
  476.9 8.0 all_gather.51
  486.6 20.1 %while.69 = (s32[]{:T(128)}, bf16[2,3,2048,64]{2,3,1,0:T(8,128)(2,1)}, bf16[2,256,8]{2,1,0:T(8,128)(2,1)S(1)}, bf16[2,256,3,256]{3,1,2,0:T(8,128)(2,1)}, bf16[2,256,3,64]{1,3,2,0:T(8,128)(2,1)}) while((s32[]{:T(128)}, bf16[2,3,2048,64]{2,3,1,0:T(8,128)(2,1)}, bf16[2,256,8]{2,1,0:T(8,128)(2,1)S(1)}, ...), condition=%wide.region_26.27_spmd.clone, body=%wide.region_25.26_spmd.sunk.clone | while | flops 207618048 | bytes 20427872 | solution.py:239
  521.8 20.7 %psum.65 = bf16[2,3,8,256]{3,2,1,0:T(8,128)(2,1)S(1)} all-reduce(bf16[2,3,8,256]{3,2,1,0:T(8,128)(2,1)S(1)} %fusion.107), channel_id=1, replica_groups=mesh['shard'=2,'ctx'=4,'tp'=4] {'ctx'}, use_global_device_ids=true, to_apply=%region_31.32 | all-reduce | flops 12288 | bytes 49152 | tf_op jit(solution)/shard_map/psum | solution.py:249
  546.9 76.6 %all-gather.9.cloned.1.call-done = bf16[8,3,2048,64]{2,3,1,0:T(8,128)(2,1)} async-done(((bf16[2,3,2048,64]{2,3,1,0:T(8,128)(2,1)}), bf16[8,3,2048,64]{2,3,1,0:T(8,128)(2,1)}) %all-gather.9.cloned.1.call-update) | async-done | bytes 6291472 | tf_op jit(solution)/shard_map/all_gather | solution.py:245
  639.5 22.2 %while.71 = (s32[]{:T(128)}, bf16[2,256,3,64]{1,3,2,0:T(8,128)(2,1)}, bf16[2,3,2048,64]{2,3,1,0:T(8,128)(2,1)S(1)}, bf16[2,256,8]{2,1,0:T(8,128)(2,1)S(1)}, bf16[2,256,3,256]{3,1,2,0:T(8,128)(2,1)}) while((s32[]{:T(128)}, bf16[2,256,3,64]{1,3,2,0:T(8,128)(2,1)}, bf16[2,3,2048,64]{2,3,1,0:T(8,128)(2,1)S(1)}, ...), condition=%wide.region_34.35_spmd.clone, body=%wide.region_33.34_spmd.sunk.clone | while | flops 202899456 | bytes 45692112 | solution.py:258
  677.5 39.9 %all-reduce = (f32[768]{0:T(1024)}, f32[768]{0:T(1024)}, f32[3072]{0:T(1024)S(1)}, f32[768]{0:T(1024)}, f32[768]{0:T(1024)}, /*index=5*/f32[768]{0:T(1024)}) all-reduce(f32[768]{0:T(1024)S(1)} %copy-done.64, f32[768]{0:T(1024)S(1)} %copy-done.63, ...), channel_id=1, replica_groups=mesh['shard'=2,'ctx'=4,'tp'=4] {'shard','ctx','tp'}, use_global_device_ids=true, to_apply=%region_41.42 | all-reduce | flops 6912 | bytes 55296 | tf_op jit(solution)/shard_map/psum | solution.py:302
  721.6 59.2 %reduce-scatter.31.cloned.1.call-done = f32[96,192]{1,0:T(8,128)} async-done(((f32[768,192]{1,0:T(8,128)}), f32[96,192]{1,0:T(8,128)}) %reduce-scatter.31.cloned.1.call-update) | async-done | bytes 73744
  780.8 73.0 %reduce-scatter.29.cloned.1.call-done = f32[768,96]{0,1:T(8,128)} async-done(((f32[768,768]{0,1:T(8,128)}), f32[768,96]{0,1:T(8,128)}) %reduce-scatter.29.cloned.1.call-update) | async-done | bytes 294928 | tf_op jit(solution)/shard_map/reduce_scatter | solution.py:295
  853.8 73.1 %reduce-scatter.27.cloned.1.call-done = f32[96,768]{1,0:T(8,128)} async-done(((f32[768,768]{1,0:T(8,128)}), f32[96,768]{1,0:T(8,128)}) %reduce-scatter.27.cloned.1.call-update) | async-done | bytes 294928 | tf_op jit(solution)/shard_map/reduce_scatter | solution.py:293
  926.9 66.5 %reduce-scatter.33.cloned.1.call-done = f32[96,192]{1,0:T(8,128)} async-done(((f32[768,192]{1,0:T(8,128)}), f32[96,192]{1,0:T(8,128)}) %reduce-scatter.33.cloned.1.call-update) | async-done | bytes 73744
  993.4 66.3 %reduce-scatter.35.cloned.1.call-done = f32[96,192]{1,0:T(8,128)} async-done(((f32[768,192]{1,0:T(8,128)}), f32[96,192]{1,0:T(8,128)}) %reduce-scatter.35.cloned.1.call-update) | async-done | bytes 73744
  (357 shorter events, 206.3 us)
Async XLA Ops:
  8.0 44.3 %copy-start = (f32[3,64,256]{2,1,0:T(8,128)S(1)}, f32[3,64,256]{2,1,0:T(8,128)}, u32[]{:S(2)}) copy-start(f32[3,64,256]{2,1,0:T(8,128)} %param.30) | copy-start | bytes 589828
  8.0 335.1 %reduce-scatter.19.cloned.1.call-start = ((), (), s32[]{:S(2)}) async-start(), calls=%async_computation.10 | async-start | bytes 1966080 | tf_op jit(solution)/shard_map/reduce_scatter | solution.py:166
  18.5 69.3 %copy-start.6 = (bf16[2,256,768]{2,1,0:T(8,128)(2,1)}, bf16[2,256,768]{2,1,0:T(8,128)(2,1)S(1)}, u32[]{:S(2)}) copy-start(bf16[2,256,768]{2,1,0:T(8,128)(2,1)S(1)} %all_gather.42) | copy-start | bytes 2359300
  150.7 97.6 %copy-start.25 = (bf16[2,256,3,256]{1,3,0,2:T(8,128)(2,1)}, bf16[2,256,3,256]{1,3,0,2:T(8,128)(2,1)S(1)}, u32[]{:S(2)}) copy-start(bf16[2,256,3,256]{1,3,0,2:T(8,128)(2,1)S(1)} %get-tuple-element.414) | copy-start | bytes 2359300
  267.6 45.3 %copy-start.48 = (f32[2,256,3,64]{1,3,2,0:T(8,128)S(1)}, f32[2,256,3,64]{1,3,2,0:T(8,128)}, u32[]{:S(2)}) copy-start(f32[2,256,3,64]{1,3,2,0:T(8,128)} %get-tuple-element.177) | copy-start | bytes 1179652
  314.6 44.4 %all-gather.5.cloned.1.call-start = ((), (), s32[]{:S(2)}) async-start(), calls=%async_computation.11 | async-start | bytes 1327104 | tf_op jit(solution)/shard_map/all_gather | solution.py:124
  315.2 43.9 %copy-start.75 = (f32[768]{0:T(1024)S(1)}, f32[768]{0:T(1024)}, u32[]{:S(2)}) copy-start(f32[768]{0:T(1024)} %param.38) | copy-start | bytes 9220
  315.2 85.6 %all-gather.7.cloned.1.call-start = ((), (), s32[]{:S(2)}) async-start(), calls=%async_computation.12 | async-start | bytes 1327104 | tf_op jit(solution)/shard_map/all_gather | solution.py:126
  315.8 114.8 %reduce-scatter.21.cloned.1.call-start = ((), (), s32[]{:S(2)}) async-start(), calls=%async_computation.13 | async-start | bytes 1966080 | tf_op jit(solution)/shard_map/reduce_scatter | solution.py:187
  344.3 132.4 %copy-start.8 = (f32[2,64,768]{2,1,0:T(8,128)}, f32[2,64,768]{2,1,0:T(8,128)S(1)}, u32[]{:S(2)}) copy-start(f32[2,64,768]{2,1,0:T(8,128)S(1)} %get-tuple-element.395) | copy-start | bytes 1179652
  344.5 132.2 %copy-start.54 = (f32[2,64]{1,0:T(2,128)}, f32[2,64]{1,0:T(2,128)S(1)}, u32[]{:S(2)}) copy-start(f32[2,64]{1,0:T(2,128)S(1)} %add_rsqrt_fusion.1) | copy-start | bytes 1540
  404.1 69.9 %reduce-scatter.23.cloned.1.call-start = ((), (), s32[]{:S(2)}) async-start(), calls=%async_computation.14 | async-start | bytes 1966080 | tf_op jit(solution)/shard_map/reduce_scatter | solution.py:219
  445.3 178.3 %all-gather.9.cloned.1.call-start = ((), (), s32[]{:S(2)}) async-start(), calls=%async_computation.18 | async-start | bytes 7864320 | tf_op jit(solution)/shard_map/all_gather | solution.py:245
  506.8 211.3 %reduce-scatter.37.cloned.1.call-start = ((), (), s32[]{:S(2)}) async-start(), calls=%async_computation.22 | async-start | bytes 884736
  545.0 82.8 %copy-start.34 = (bf16[2,256,3,64]{1,3,2,0:T(8,128)(2,1)}, bf16[2,256,3,64]{1,3,2,0:T(8,128)(2,1)S(1)}, u32[]{:S(2)}) copy-start(bf16[2,256,3,64]{1,3,2,0:T(8,128)(2,1)S(1)} %fusion.96) | copy-start | bytes 589828
  546.7 173.0 %reduce-scatter.25.cloned.1.call-start = ((), (), s32[]{:S(2)}) async-start(), calls=%async_computation.15 | async-start | bytes 983040 | tf_op jit(solution)/shard_map/reduce_scatter | solution.py:274
  665.2 115.6 %reduce-scatter.31.cloned.1.call-start = ((), (), s32[]{:S(2)}) async-start(), calls=%async_computation.19 | async-start | bytes 884736
  666.8 187.0 %reduce-scatter.29.cloned.1.call-start = ((), (), s32[]{:S(2)}) async-start(), calls=%async_computation.17 | async-start | bytes 2654208 | tf_op jit(solution)/shard_map/reduce_scatter | solution.py:295
  669.2 257.7 %reduce-scatter.27.cloned.1.call-start = ((), (), s32[]{:S(2)}) async-start(), calls=%async_computation.16 | async-start | bytes 2654208 | tf_op jit(solution)/shard_map/reduce_scatter | solution.py:293
  672.8 320.6 %reduce-scatter.33.cloned.1.call-start = ((), (), s32[]{:S(2)}) async-start(), calls=%async_computation.20 | async-start | bytes 884736
  675.2 384.4 %reduce-scatter.35.cloned.1.call-start = ((), (), s32[]{:S(2)}) async-start(), calls=%async_computation.21 | async-start | bytes 884736
  675.9 43.8 %copy-start.9 = (f32[2,64,768]{2,1,0:T(8,128)S(1)}, f32[2,64,768]{2,1,0:T(8,128)}, u32[]{:S(2)}) copy-start(f32[2,64,768]{2,1,0:T(8,128)} %copy-done.8) | copy-start | bytes 1179652
  675.9 43.8 %copy-start.22 = (f32[2,64,768]{2,1,0:T(8,128)S(1)}, f32[2,64,768]{2,1,0:T(8,128)}, u32[]{:S(2)}) copy-start(f32[2,64,768]{2,1,0:T(8,128)} %copy-done.21) | copy-start | bytes 1179652
  676.0 43.8 %copy-start.55 = (f32[2,64]{1,0:T(2,128)S(1)}, f32[2,64]{1,0:T(2,128)}, u32[]{:S(2)}) copy-start(f32[2,64]{1,0:T(2,128)} %copy-done.54) | copy-start | bytes 1540
  (74 other events, 622.4 us)
Sparse Core Ops, SparseCore 0:
  314.7 28.4 reduce-scatter.18
  404.2 26.3 reduce-scatter.20
  445.4 28.5 reduce-scatter.22
Sparse Core Ops, SparseCore 1:
  317.2 41.8 all-gather.4
  361.0 39.7 all-gather.6
  506.8 116.7 all-gather.8
  626.9 61.6 reduce-scatter.36
  691.1 22.2 reduce-scatter.24
  717.3 63.4 reduce-scatter.30
  784.7 69.0 reduce-scatter.28
  857.7 69.1 reduce-scatter.26
  930.7 62.7 reduce-scatter.32
  997.3 62.3 reduce-scatter.34
